TPU v7x, 128 devices: a whole 4x4x4 slice. The times are simulated.
128 devices in a mesh: head: 4 (over z_lo, core), tok: 32 (over x, z_hi, y).
Axes of the slice: x: 4, y: 4, z: 4 (z_hi: 2, z_lo: 2; z = z_hi * 2 + z_lo), core: 2. Of those that a mesh axis runs over, the one named last changes fastest.
Arguments:
- hidden_in: bfloat16 [8192, 2048], P('tok'), may hold values from -6 to 6
- queries: bfloat16 [8192, 2048], P('tok', 'head'), may hold values from -4.5 to 4.5
- keys: bfloat16 [8192, 2048], P('tok', 'head'), may hold values from -4.5 to 4.5
- values: bfloat16 [8192, 2048], P('tok', 'head'), may hold values from -6 to 6
- request_ids: int32 [8192], replicated, may hold values from 0 to 63, never falling along the last dimension, each value on 1 to 1024 neighbouring positions
- out_proj: bfloat16 [2048, 2048], P('head'), may hold values from -0.125 to 0.125
- norm_gain: float32 [2048], replicated, may hold values from 0.1 to 1.9
- expert_gate_up: bfloat16 [32, 2048, 2, 1408], P('tok', None, None, 'head'), may hold values from -0.125 to 0.125
- expert_down: bfloat16 [32, 1408, 2048], P('tok', 'head'), may hold values from -0.15625 to 0.15625
- shared_gate_up: bfloat16 [2048, 2, 2816], P(None, None, 'head'), may hold values from -0.125 to 0.125
- shared_down: bfloat16 [2816, 2048], P('head'), may hold values from -0.109375 to 0.109375
- shared_gate: bfloat16 [2048], replicated, may hold values from -0.125 to 0.125
- routes: int32 [8192, 4], P('tok'), may hold values from 0 to 31, all different within a row; in each aligned block of 256 rows (0 to 255, 256 to 511, ...) at most 48 rows name the same one
- route_weights: float32 [8192, 4], P('tok'), may hold values from 0.05 to 0.5
- page_slots: int32 [1024], replicated, may hold values from 0 to 1023, as said below
Outputs:
- layer_out: bfloat16 [8192, 2048], P('tok', 'head')
- decode_cache: bfloat16 [1024, 8, 4096], P('tok', 'head')
Inputs may be any that keep to these rules, and one draw needn't show every extreme that they name: `request_ids`: ids never fall along the tokens; each request holds 1 to 1024 consecutive tokens, and one holds exactly 1024. `routes`: each row names 4 different experts; among the rows of one device no expert is named more than 48 times, a bound that some block reaches. `page_slots`: a permutation; for any two aligned blocks, one of 32 pages and one of 32 cache rows, the number of pages of the first that go to rows of the second is exactly 1.
All inputs are finite; a program needn't handle non-finite values.
Results may differ from a plain program's by a relative error of at most 0.0065.
Values may be sent and summed in bfloat16 or wider, within the bound.
No kernel may reach another device: no remote copies, remote signals or barrier semaphores. Data moves between devices by JAX's collectives and lax.ppermute only.
A program may use at most 128 MiB of HBM per device.

v0:
```python
import math
import jax
import jax.numpy as jnp
from jax import lax
from jax.sharding import PartitionSpec as P

HD = 128
TOP = 4
EXPERTS = 32
PAGE = 8
REACH = 4
CAP = 48


def from_behind(value, axis, steps):
    count = lax.axis_size(axis)
    leading, last = (max(0, -steps), min(count, count - steps))
    return lax.ppermute(value, axis, [(source, source + steps) for source in range(leading, last)])


def run_experts(slots, gate_up, down):
    both = jnp.einsum("secd,edgf->secgf", slots, gate_up, preferred_element_type=jnp.float32)
    active = (jax.nn.silu(both[..., 0, :]) * both[..., 1, :]).astype(jnp.bfloat16)
    return jnp.einsum("secf,efd->secd", active, down, preferred_element_type=jnp.float32)


def per_device(
    hidden_in,
    queries,
    keys,
    values,
    request_ids,
    out_proj,
    norm_gain,
    expert_gate_up,
    expert_down,
    shared_gate_up,
    shared_down,
    shared_gate,
    routes,
    route_weights,
    page_slots,
):
    tok_rows = hidden_in.shape[0]
    model_width = hidden_in.shape[1]
    head_width = queries.shape[1]
    heads_here = head_width // HD
    tok_count = lax.axis_size("tok")
    head_count = lax.axis_size("head")
    tok_index = lax.axis_index("tok")
    head_index = lax.axis_index("head")
    column_width = model_width // head_count
    key_list = [keys]
    value_list = [values]
    for step in range(1, REACH + 1):
        far_keys, far_values = from_behind((keys, values), "tok", step)
        key_list.insert(0, far_keys)
        value_list.insert(0, far_values)
    span = REACH * tok_rows
    window_keys = jnp.concatenate(key_list, 0).reshape(span + tok_rows, heads_here, HD)
    window_values = jnp.concatenate(value_list, 0).reshape(span + tok_rows, heads_here, HD)
    padded_ids = jnp.concatenate([jnp.full((span,), -1, jnp.int32), request_ids], 0)
    base = tok_index * tok_rows
    key_ids = lax.dynamic_slice_in_dim(padded_ids, base, span + tok_rows, 0)
    query_ids = lax.dynamic_slice_in_dim(request_ids, base, tok_rows, 0)
    query_pos = jnp.arange(tok_rows, dtype=jnp.int32) + span
    key_pos = jnp.arange(span + tok_rows, dtype=jnp.int32)
    allowed = (query_ids[:, None] == key_ids[None, :]) & (key_pos[None, :] <= query_pos[:, None])
    scores = jnp.einsum(
        "qhd,khd->hqk",
        queries.reshape(tok_rows, heads_here, HD),
        window_keys,
        preferred_element_type=jnp.float32,
    ) * (1.0 / math.sqrt(HD))
    scores = jnp.where(allowed[None], scores, -1e30)
    top = jnp.max(scores, axis=-1, keepdims=True)
    weights = jnp.exp(scores - top)
    probs = (weights / jnp.sum(weights, axis=-1, keepdims=True)).astype(jnp.bfloat16)
    attended = (
        jnp.einsum("hqk,khd->qhd", probs, window_values, preferred_element_type=jnp.float32)
        .astype(jnp.bfloat16)
        .reshape(tok_rows, head_width)
    )
    projected = jnp.dot(attended, out_proj, preferred_element_type=jnp.float32)
    total = lax.psum(projected, "head")
    resid = hidden_in.astype(jnp.float32) + total
    mean_square = jnp.mean(resid * resid, axis=-1, keepdims=True)
    normed = (resid * lax.rsqrt(mean_square + 1e-06) * norm_gain).astype(jnp.bfloat16)
    resid_cols = lax.dynamic_slice_in_dim(resid, head_index * column_width, column_width, 1)
    shared_both = jnp.einsum(
        "td,dgf->tgf", normed, shared_gate_up, preferred_element_type=jnp.float32
    )
    shared_act = (jax.nn.silu(shared_both[:, 0, :]) * shared_both[:, 1, :]).astype(jnp.bfloat16)
    shared_scale = jax.nn.sigmoid(jnp.dot(normed, shared_gate, preferred_element_type=jnp.float32))
    shared_term = shared_scale[:, None] * jnp.dot(
        shared_act, shared_down, preferred_element_type=jnp.float32
    )
    flat_routes = routes.reshape(-1)
    assign = tok_rows * TOP
    expert_ids = jnp.arange(EXPERTS, dtype=jnp.int32)
    onehot = (flat_routes[:, None] == expert_ids[None, :]).astype(jnp.int32)
    before = jnp.cumsum(onehot, 0) - onehot
    rank = jnp.sum(before * onehot, 1)
    slot = flat_routes * CAP + rank
    source_row = (
        jnp.zeros((EXPERTS * CAP,), jnp.int32)
        .at[slot]
        .set(jnp.arange(assign, dtype=jnp.int32) // TOP)
    )
    filled = jnp.zeros((EXPERTS * CAP,), jnp.bool_).at[slot].set(True)
    outgoing = jnp.where(filled[:, None], normed[source_row], jnp.zeros((), jnp.bfloat16))
    local_experts = EXPERTS // tok_count
    outgoing = outgoing.reshape(tok_count, local_experts, CAP, model_width)
    partial_value = run_experts(
        lax.all_to_all(outgoing, "tok", split_axis=0, concat_axis=0, tiled=True),
        expert_gate_up,
        expert_down,
    )
    flat_weights = route_weights.reshape(tok_rows, TOP, 1)
    slot_cols, shared_cols = (
        lax.psum_scatter(
            partial_value.reshape(EXPERTS * CAP, model_width),
            "head",
            scatter_dimension=1,
            tiled=True,
        ),
        lax.psum_scatter(shared_term, "head", scatter_dimension=1, tiled=True),
    )
    returned = lax.all_to_all(
        slot_cols.reshape(tok_count, local_experts * CAP, column_width).astype(jnp.bfloat16),
        "tok",
        split_axis=0,
        concat_axis=0,
        tiled=True,
    ).astype(jnp.float32)
    picked = returned.reshape(EXPERTS * CAP, column_width)[slot].reshape(
        tok_rows, TOP, column_width
    )
    moe_cols = jnp.sum(picked * flat_weights, 1)
    layer_cols = resid_cols + shared_cols + moe_cols
    layer_out = layer_cols.astype(jnp.bfloat16)
    pages_here = tok_rows // PAGE
    pair = pages_here // tok_count
    quarter_page = PAGE // head_count
    slots_all = page_slots.reshape(tok_count, pages_here)
    owner_all = slots_all // pages_here
    same_owner = owner_all[:, :, None] == owner_all[:, None, :]
    earlier = slots_all[:, None, :] < slots_all[:, :, None]
    rank_all = jnp.sum((same_owner & earlier).astype(jnp.int32), 2)
    send_pos = owner_all * pair + rank_all
    mine_pos = lax.dynamic_index_in_dim(send_pos, tok_index, 0, keepdims=False)
    page_ids = jnp.arange(pages_here, dtype=jnp.int32)
    send_order = jnp.zeros((pages_here,), jnp.int32).at[mine_pos].set(page_ids)
    sources = jnp.arange(tok_count, dtype=jnp.int32)[:, None]
    target = jnp.where(owner_all == tok_index, sources * pair + rank_all, pages_here)
    arrival_slot = (
        jnp.zeros((pages_here + 1,), jnp.int32)
        .at[target.reshape(-1)]
        .set((slots_all % pages_here).reshape(-1))[:pages_here]
    )
    place_order = jnp.zeros((pages_here,), jnp.int32).at[arrival_slot].set(page_ids)
    kv_pages = jnp.stack([keys, values], 1).reshape(
        pages_here, head_count, quarter_page, 2, heads_here, HD
    )[send_order]
    row_width = 2 * head_count * heads_here * HD
    spread = kv_pages.reshape(
        tok_count, pair, head_count, quarter_page, 2, heads_here, HD
    ).transpose(2, 0, 1, 3, 4, 5, 6)
    spread = spread.reshape(head_count * tok_count, pair, quarter_page, 2, heads_here, HD)
    landed = lax.all_to_all(spread, ("head", "tok"), split_axis=0, concat_axis=0, tiled=True)
    landed = landed.reshape(head_count, tok_count, pair, quarter_page, 2, heads_here, HD).transpose(
        1, 2, 3, 4, 0, 5, 6
    )
    landed = landed.reshape(pages_here, quarter_page, row_width)
    decode_cache = landed[place_order]
    return (layer_out, decode_cache)


def solution(mesh):
    in_specs = (
        P("tok", None),
        P("tok", "head"),
        P("tok", "head"),
        P("tok", "head"),
        P(),
        P("head", None),
        P(),
        P("tok", None, None, "head"),
        P("tok", "head", None),
        P(None, None, "head"),
        P("head", None),
        P(),
        P("tok", None),
        P("tok", None),
        P(),
    )
    out_specs = (P("tok", "head"), P("tok", "head", None))
    return jax.shard_map(
        per_device, mesh=mesh, in_specs=in_specs, out_specs=out_specs, check_vma=False
    )
```

profile of v0, /device:TPU:8, one launch (start us, length us, event | category | flops | bytes accessed | tf_op | source)
XLA Modules:
  0.0 430.8 jit_solution(11822778492569103594)
XLA Ops:
  8.5 5.8 %collective-permute-start.4 = (bf16[256,512]{0,1:T(8,128)(2,1)S(1)}, bf16[256,512]{0,1:T(8,128)(2,1)S(1)}, u32[]{:S(2)}, u32[]{:S(2)}) collective-permute-start(bf16[256,512]{0,1:T(8,128)(2,1)S(1)} %copy.77), channel_id=1, source_target_pairs={{0,4},{1,5},{2,6},{3,7},{4,8},{5,9},{6,10},{7,11},{8,12},{9,13},{1... | collective-permute-start | bytes 786440 | tf_op jit(solution)/shard_map/ppermute | solution.py:18
  14.3 3.1 collective-permute-start.5
  17.3 4.5 %collective-permute-start.6 = (bf16[256,512]{0,1:T(8,128)(2,1)S(1)}, bf16[256,512]{0,1:T(8,128)(2,1)}, u32[]{:S(2)}, u32[]{:S(2)}) collective-permute-start(bf16[256,512]{0,1:T(8,128)(2,1)S(1)} %copy.77), channel_id=1, source_target_pairs={{0,2},{1,3},{2,4},{3,5},{4,6},{5,7},{6,8},{7,9},{8,10},{9,11},{10,... | collective-permute-start | bytes 786440 | tf_op jit(solution)/shard_map/ppermute | solution.py:18
  21.8 3.1 collective-permute-start.7
  25.0 6.5 %collective-permute-start = (bf16[256,512]{1,0:T(8,128)(2,1)}, bf16[256,512]{1,0:T(8,128)(2,1)}, u32[]{:S(2)}, u32[]{:S(2)}) collective-permute-start(bf16[256,512]{1,0:T(8,128)(2,1)} %param.18), channel_id=1, source_target_pairs={{0,4},{1,5},{2,6},{3,7},{4,8},{5,9},{6,10},{7,11},{8,12},{9,13},{1... | collective-permute-start | bytes 786440 | tf_op jit(solution)/shard_map/ppermute | solution.py:18
  34.0 9.6 %collective-permute-start.1 = (bf16[256,512]{1,0:T(8,128)(2,1)}, bf16[256,512]{1,0:T(8,128)(2,1)S(1)}, u32[]{:S(2)}, u32[]{:S(2)}) collective-permute-start(bf16[256,512]{1,0:T(8,128)(2,1)} %param.18), channel_id=1, source_target_pairs={{0,3},{1,4},{2,5},{3,6},{4,7},{5,8},{6,9},{7,10},{8,11},{9,12},{10... | collective-permute-start | bytes 786440 | tf_op jit(solution)/shard_map/ppermute | solution.py:18
  46.1 4.0 collective-permute-start.3
  56.9 2.4 copy.76
  59.3 3.5 exponential_reduce_fusion
  62.8 4.5 %fusion.15 = bf16[4,128,256]{2,1,0:T(8,128)(2,1)S(1)} fusion(bf16[1280,4,128]{0,2,1:T(8,128)(2,1)} %bitcast.151, f32[4,256]{1,0:T(4,128)S(1)} %exponential_reduce_fusion, bf16[1280,4,128]{0,2,1:T(8,128)(2,1)} %bitcast.155, pred[256,1280]{0,1:T(8,128)(4,1)} %fusion.14, bf16[256,512]{1,0:T(8,128)(2,1)} %param.16), kind=kOutput, calls=%fused_computation.32 | convolution fusion | flops 677775616 | bytes 3477504 | tf_op jit(solution)/shard_map/hqk,khd->qhd/dot_general | solution.py:80
  67.3 3.6 fusion.75
  72.0 9.0 %reduce-window.6 = s32[32,8,128]{2,1,0:T(8,128)S(1)} reduce-window(s32[32,8,128]{2,1,0:T(8,128)S(1)} %fusion.42, s32[]{:T(128)} %constant.46.clone.1), window={size=1x1x128 pad=0_0x0_0x127_0}, to_apply=%region_5.6 | reduce-window | flops 4161536 | bytes 262148 | tf_op jit(solution)/shard_map/reduce-window
  81.8 4.5 %scatter_custom_fusion.1 = s32[1536]{0:T(1024)S(1)} fusion(s32[1024]{0:T(1024)S(1)} %bitcast.158, s32[1024]{0:T(1024)S(1)} %add_select_fusion.3, s32[]{:T(128)} %constant.46.clone.1), kind=kCustom, calls=%fused_computation.98 | custom fusion | bytes 6148 | tf_op jit(solution)/shard_map/scatter | solution.py:108
  86.3 4.3 %scatter_custom_fusion = pred[1536]{0:T(1024)(128)(4,1)S(1)} fusion(s32[1024]{0:T(1024)S(1)} %bitcast.159, pred[1024]{0:T(1024)(128)(4,1)S(1)} %broadcast.250, pred[]{:T(512)} %constant.99.clone.1), kind=kCustom, calls=%fused_computation.102 | custom fusion | bytes 1537 | tf_op jit(solution)/shard_map/scatter | solution.py:110
  90.8 46.8 %all-reduce.3.cloned.1.call-done = f32[256,2048]{1,0:T(8,128)} async-done(((f32[256,2048]{1,0:T(8,128)}), f32[256,2048]{1,0:T(8,128)}) %all-reduce.3.cloned.1.call-update) | async-done | bytes 2097168 | tf_op jit(solution)/shard_map/psum | solution.py:85
  142.3 14.1 %gather_fusion = bf16[1536,2048]{1,0:T(8,128)(2,1)} fusion(bf16[256,2048]{1,0:T(8,128)(2,1)} %multiply_convert_fusion, s32[2048]{0:T(1024)S(1)} %pad_clamp_fusion), kind=kCustom, calls=%fused_computation | custom fusion | bytes 12589056 | tf_op jit(solution)/shard_map/gather | solution.py:111
  156.4 3.3 broadcast_select_fusion
  159.7 83.4 %all_to_all.15 = bf16[32,1,48,2048]{3,2,1,0:T(8,128)(2,1)S(1)} all-to-all(bf16[32,1,48,2048]{3,2,1,0:T(8,128)(2,1)S(1)} %broadcast_select_fusion), channel_id=1, replica_groups=mesh['head'=4,'tok'=32] {'tok'}, dimensions={0} | all-to-all | bytes 12582912 | tf_op jit(solution)/shard_map/all_to_all | solution.py:115
  243.1 5.2 %fusion.7 = f32[32,1,48,2,352]{4,2,3,0,1:T(8,128)S(1)} fusion(bf16[1,2048,2,352]{1,3,2,0:T(8,128)(2,1)S(1)} %copy-done, bf16[32,1,48,2048]{3,2,1,0:T(8,128)(2,1)S(1)} %all_to_all.15), kind=kOutput, calls=%fused_computation.22 | convolution fusion | flops 4429185024 | bytes 13500416 | tf_op jit(solution)/shard_map/secd,edgf->secgf/dot_general | solution.py:22
  248.3 6.4 %fusion.12 = f32[32,48,2048]{2,1,0:T(8,128)} fusion(bf16[1,352,2048]{2,1,0:T(8,128)(2,1)S(1)} %copy-done.13, f32[32,1,48,2,352]{4,2,3,0,1:T(8,128)S(1)} %fusion.7), kind=kOutput, calls=%fused_computation.28 | convolution fusion | flops 2217836544 | bytes 18350080 | tf_op jit(solution)/shard_map/secf,efd->secd/dot_general | solution.py:24
  256.4 4.5 %fusion.18 = f32[256,2,704]{0,2,1:T(8,128)S(1)} fusion(bf16[2048,2,704]{0,2,1:T(8,128)(2,1)} %param.24, bf16[256,2048]{1,0:T(8,128)(2,1)S(1)} %copy-done.2), kind=kOutput, calls=%fused_computation.34 | convolution fusion | flops 1476395008 | bytes 8257536 | tf_op jit(solution)/shard_map/td,dgf->tgf/dot_general | solution.py:90
  260.9 2.4 convolution_multiply_fusion
  265.2 4.3 scatter_custom_fusion.3
  273.5 4.5 %all-to-all-start.2 = ((bf16[128,1,2,2,4,128]{5,4,3,2,1,0:T(4,128)(2,1)}), bf16[128,1,2,2,4,128]{5,4,3,2,1,0:T(4,128)(2,1)S(1)}, u32[]{:S(2)}, u32[]{:S(2)}) async-start(bf16[128,1,2,2,4,128]{5,4,3,2,1,0:T(4,128)(2,1)} %copy.93), calls=%async_computation.4 | async-start | bytes 1048576 | tf_op jit(solution)/shard_map/all_to_all | solution.py:170
  278.0 92.0 %reduce-scatter.5.cloned.1.call-done = f32[1536,512]{1,0:T(8,128)} async-done(((f32[1536,2048]{1,0:T(8,128)}), f32[1536,512]{1,0:T(8,128)}) %reduce-scatter.5.cloned.1.call-update) | async-done | bytes 3145744 | tf_op jit(solution)/shard_map/reduce_scatter | solution.py:121
  370.0 3.2 convert_element_type.57
  373.3 9.8 %all-to-all-start.1 = ((bf16[32,48,512]{2,1,0:T(8,128)(2,1)}), bf16[32,48,512]{2,1,0:T(8,128)(2,1)S(1)}, u32[]{:S(2)}, u32[]{:S(2)}) async-start(bf16[32,48,512]{2,1,0:T(8,128)(2,1)} %bitcast.32), calls=%async_computation.3 | async-start | bytes 3145728 | tf_op jit(solution)/shard_map/all_to_all | solution.py:129
  384.4 2.4 gather_fusion.3
  386.8 20.0 %all-to-all-done.1 = bf16[32,48,512]{2,1,0:T(8,128)(2,1)S(1)} async-done(((bf16[32,48,512]{2,1,0:T(8,128)(2,1)}), bf16[32,48,512]{2,1,0:T(8,128)(2,1)S(1)}, u32[]{:S(2)}, u32[]{:S(2)}) %all-to-all-start.1) | async-done | bytes 1572896 | tf_op jit(solution)/shard_map/all_to_all | solution.py:129
  409.0 7.2 %gather_fusion.1 = f32[1024,512]{1,0:T(8,128)} fusion(f32[1536,512]{1,0:T(8,128)} %bitcast_convert_fusion, s32[1024]{0:T(1024)S(1)} %broadcast_clamp_fusion), kind=kCustom, calls=%fused_computation.1 | custom fusion | bytes 4198400 | tf_op jit(solution)/shard_map/gather | solution.py:136
  416.2 3.1 reshape.311
  419.3 2.9 multiply_reduce_fusion
  (116 shorter events, 32.6 us)
Async XLA Ops:
  7.2 236.0 %copy-start = (bf16[1,2048,2,352]{1,3,2,0:T(8,128)(2,1)S(1)}, bf16[1,2048,2,352]{1,3,2,0:T(8,128)(2,1)}, u32[]{:S(2)}) copy-start(bf16[1,2048,2,352]{1,3,2,0:T(8,128)(2,1)} %param.22) | copy-start | bytes 8650756
  7.2 130.4 %all-reduce.3.cloned.1.call-start = ((), (), s32[]{:S(2)}) async-start(), calls=%async_computation.5 | async-start | bytes 4194304 | tf_op jit(solution)/shard_map/psum | solution.py:85
  8.5 25.6 %collective-permute-start.4 = (bf16[256,512]{0,1:T(8,128)(2,1)S(1)}, bf16[256,512]{0,1:T(8,128)(2,1)S(1)}, u32[]{:S(2)}, u32[]{:S(2)}) collective-permute-start(bf16[256,512]{0,1:T(8,128)(2,1)S(1)} %copy.77), channel_id=1, source_target_pairs={{0,4},{1,5},{2,6},{3,7},{4,8},{5,9},{6,10},{7,11},{8,12},{9,13},{1... | collective-permute-start | bytes 786440 | tf_op jit(solution)/shard_map/ppermute | solution.py:18
  14.3 29.4 %collective-permute-start.5 = (bf16[256,512]{0,1:T(8,128)(2,1)S(1)}, bf16[256,512]{0,1:T(8,128)(2,1)}, u32[]{:S(2)}, u32[]{:S(2)}) collective-permute-start(bf16[256,512]{0,1:T(8,128)(2,1)S(1)} %copy.77), channel_id=1, source_target_pairs={{0,3},{1,4},{2,5},{3,6},{4,7},{5,8},{6,9},{7,10},{8,11},{9,12},{10... | collective-permute-start | bytes 786440 | tf_op jit(solution)/shard_map/ppermute | solution.py:18
  17.3 28.7 %collective-permute-start.6 = (bf16[256,512]{0,1:T(8,128)(2,1)S(1)}, bf16[256,512]{0,1:T(8,128)(2,1)}, u32[]{:S(2)}, u32[]{:S(2)}) collective-permute-start(bf16[256,512]{0,1:T(8,128)(2,1)S(1)} %copy.77), channel_id=1, source_target_pairs={{0,2},{1,3},{2,4},{3,5},{4,6},{5,7},{6,8},{7,9},{8,10},{9,11},{10,... | collective-permute-start | bytes 786440 | tf_op jit(solution)/shard_map/ppermute | solution.py:18
  21.8 29.2 %collective-permute-start.7 = (bf16[256,512]{0,1:T(8,128)(2,1)S(1)}, bf16[256,512]{0,1:T(8,128)(2,1)}, u32[]{:S(2)}, u32[]{:S(2)}) collective-permute-start(bf16[256,512]{0,1:T(8,128)(2,1)S(1)} %copy.77), channel_id=1, source_target_pairs={{0,1},{1,2},{2,3},{3,4},{4,5},{5,6},{6,7},{7,8},{8,9},{9,10},{10,1... | collective-permute-start | bytes 786440 | tf_op jit(solution)/shard_map/ppermute | solution.py:18
  25.0 27.1 %collective-permute-start = (bf16[256,512]{1,0:T(8,128)(2,1)}, bf16[256,512]{1,0:T(8,128)(2,1)}, u32[]{:S(2)}, u32[]{:S(2)}) collective-permute-start(bf16[256,512]{1,0:T(8,128)(2,1)} %param.18), channel_id=1, source_target_pairs={{0,4},{1,5},{2,6},{3,7},{4,8},{5,9},{6,10},{7,11},{8,12},{9,13},{1... | collective-permute-start | bytes 786440 | tf_op jit(solution)/shard_map/ppermute | solution.py:18
  34.0 19.9 %collective-permute-start.1 = (bf16[256,512]{1,0:T(8,128)(2,1)}, bf16[256,512]{1,0:T(8,128)(2,1)S(1)}, u32[]{:S(2)}, u32[]{:S(2)}) collective-permute-start(bf16[256,512]{1,0:T(8,128)(2,1)} %param.18), channel_id=1, source_target_pairs={{0,3},{1,4},{2,5},{3,6},{4,7},{5,8},{6,9},{7,10},{8,11},{9,12},{10... | collective-permute-start | bytes 786440 | tf_op jit(solution)/shard_map/ppermute | solution.py:18
  43.6 12.5 %copy-start.4 = (bf16[256,512]{1,0:T(8,128)(2,1)S(1)}, bf16[256,512]{1,0:T(8,128)(2,1)}, u32[]{:S(2)}) copy-start(bf16[256,512]{1,0:T(8,128)(2,1)} %param.18) | copy-start | bytes 786436
  43.6 11.0 %collective-permute-start.2 = (bf16[256,512]{1,0:T(8,128)(2,1)}, bf16[256,512]{1,0:T(8,128)(2,1)S(1)}, u32[]{:S(2)}, u32[]{:S(2)}) collective-permute-start(bf16[256,512]{1,0:T(8,128)(2,1)} %param.18), channel_id=1, source_target_pairs={{0,2},{1,3},{2,4},{3,5},{4,6},{5,7},{6,8},{7,9},{8,10},{9,11},{10,... | collective-permute-start | bytes 786440 | tf_op jit(solution)/shard_map/ppermute | solution.py:18
  46.1 9.3 %collective-permute-start.3 = (bf16[256,512]{1,0:T(8,128)(2,1)}, bf16[256,512]{1,0:T(8,128)(2,1)S(1)}, u32[]{:S(2)}, u32[]{:S(2)}) collective-permute-start(bf16[256,512]{1,0:T(8,128)(2,1)} %param.18), channel_id=1, source_target_pairs={{0,1},{1,2},{2,3},{3,4},{4,5},{5,6},{6,7},{7,8},{8,9},{9,10},{10,1... | collective-permute-start | bytes 786440 | tf_op jit(solution)/shard_map/ppermute | solution.py:18
  52.0 4.1 copy-start.6
  54.7 4.6 %copy-start.14 = (bf16[256,512]{1,0:T(8,128)(2,1)S(1)}, bf16[256,512]{1,0:T(8,128)(2,1)}, u32[]{:S(2)}) copy-start(bf16[256,512]{1,0:T(8,128)(2,1)} %param.16) | copy-start | bytes 786436
  70.9 0.7 copy-start.7
  70.9 299.1 %reduce-scatter.5.cloned.1.call-start = ((), (), s32[]{:S(2)}) async-start(), calls=%async_computation.7 | async-start | bytes 15728640 | tf_op jit(solution)/shard_map/reduce_scatter | solution.py:121
  90.8 50.3 %copy-start.9 = (f32[2048]{0:T(1024)S(1)}, f32[2048]{0:T(1024)}, u32[]{:S(2)}) copy-start(f32[2048]{0:T(1024)} %param.21) | copy-start | bytes 24580
  139.8 1.3 copy-start.3
  243.1 5.2 %copy-start.13 = (bf16[1,352,2048]{2,1,0:T(8,128)(2,1)S(1)}, bf16[1,352,2048]{2,1,0:T(8,128)(2,1)}, u32[]{:S(2)}) copy-start(bf16[1,352,2048]{2,1,0:T(8,128)(2,1)} %param.23) | copy-start | bytes 4325380
  254.7 0.7 copy-start.10
  254.8 0.7 copy-start.8
  254.8 1.3 copy-start.2
  254.8 167.5 %reduce-scatter.3.cloned.1.call-start = ((), (), s32[]{:S(2)}) async-start(), calls=%async_computation.6 | async-start | bytes 2621440 | tf_op jit(solution)/shard_map/reduce_scatter | solution.py:127
  256.4 4.5 %copy-start.12 = (bf16[704,2048]{1,0:T(8,128)(2,1)S(1)}, bf16[704,2048]{1,0:T(8,128)(2,1)}, u32[]{:S(2)}) copy-start(bf16[704,2048]{1,0:T(8,128)(2,1)} %param.25) | copy-start | bytes 8650756
  263.3 1.0 copy-start.5
  273.5 99.8 %all-to-all-start.2 = ((bf16[128,1,2,2,4,128]{5,4,3,2,1,0:T(4,128)(2,1)}), bf16[128,1,2,2,4,128]{5,4,3,2,1,0:T(4,128)(2,1)S(1)}, u32[]{:S(2)}, u32[]{:S(2)}) async-start(bf16[128,1,2,2,4,128]{5,4,3,2,1,0:T(4,128)(2,1)} %copy.93), calls=%async_computation.4 | async-start | bytes 1048576 | tf_op jit(solution)/shard_map/all_to_all | solution.py:170
  373.2 9.9 %copy-start.11 = (f32[256,4]{0,1:T(4,128)S(1)}, f32[256,4]{0,1:T(4,128)}, u32[]{:S(2)}) copy-start(f32[256,4]{0,1:T(4,128)} %param.28) | copy-start | bytes 12292
  373.3 33.5 %all-to-all-start.1 = ((bf16[32,48,512]{2,1,0:T(8,128)(2,1)}), bf16[32,48,512]{2,1,0:T(8,128)(2,1)S(1)}, u32[]{:S(2)}, u32[]{:S(2)}) async-start(bf16[32,48,512]{2,1,0:T(8,128)(2,1)} %bitcast.32), calls=%async_computation.3 | async-start | bytes 3145728 | tf_op jit(solution)/shard_map/all_to_all | solution.py:129
  416.2 8.1 %copy-start.1 = (bf16[1,2048,2,352]{1,3,2,0:T(8,128)(2,1)S(1)}, bf16[1,2048,2,352]{1,3,2,0:T(8,128)(2,1)}, u32[]{:S(2)}) copy-start(bf16[1,2048,2,352]{1,3,2,0:T(8,128)(2,1)} %param.22) | copy-start | bytes 8650756
Sparse Core Ops, SparseCore 0:
  71.0 66.4 all-reduce.2
  254.9 115.0 reduce-scatter.4
  372.5 46.0 reduce-scatter.2
where the time goes:
time: 432 us; the launch traced here: 431 us
  waiting for transfers between devices  159 us (37%)
  blocking collectives  83.4 us (19%)
  local copies, waits for them, and re-layouts  62.6 us (14%)
  starting transfers between devices  52.4 us (12%)
  matrix products  30.5 us (7%)
  other arithmetic  28.8 us (7%)
  between operations  14.3 us (3%)
    reduce_scatter x1, waiting for transfers between devices, per_device(): lax.psum_scatter(partial_value.reshape(EXPERTS * CAP, model_width), 'head...  92 us
    all_to_all x1, blocking collectives, per_device(): lax.all_to_all(outgoing, 'tok', split_axis=0, concat_axis=0, tiled=True)  83.4 us
    psum x1, waiting for transfers between devices, per_device(): total = lax.psum(projected, 'head')  46.8 us
    ppermute x8, starting transfers between devices, from_behind(): lax.ppermute(value, axis, [(source, source + steps) for source in range(l...  37.9 us
    all_to_all x1, waiting for transfers between devices, per_device(): lax.all_to_all(slot_cols.reshape(tok_count, local_experts * CAP, column_w...  20 us
    gather x1, local copies, waits for them, and re-layouts, per_device(): normed[source_row]  14.1 us
    unnamed x42, local copies, waits for them, and re-layouts  11.6 us
    all_to_all x1, starting transfers between devices, per_device(): lax.all_to_all(slot_cols.reshape(tok_count, local_experts * CAP, column_w...  9.84 us
  transfers between devices with their start and end apart: 13, of which 3 were waited for; matrix products, arithmetic and copies ran while one was open for 16% of the time, Pallas kernels for 0%

commit v1 on v0

--- a/solution.py
+++ b/solution.py
@@ -82,7 +82,7 @@
         .reshape(tok_rows, head_width)
     )
     projected = jnp.dot(attended, out_proj, preferred_element_type=jnp.float32)
-    total = lax.psum(projected, "head")
+    total = jnp.sum(lax.all_gather(projected, "head"), axis=0)
     resid = hidden_in.astype(jnp.float32) + total
     mean_square = jnp.mean(resid * resid, axis=-1, keepdims=True)
     normed = (resid * lax.rsqrt(mean_square + 1e-06) * norm_gain).astype(jnp.bfloat16)

time: 432 us -> 471 us (1.090); the launches traced: 431 us -> 464 us
  waiting for transfers between devices: 159 us -> 181 us
  other arithmetic: 28.8 us -> 34.6 us
    all_gather x0 -> x1, waiting for transfers between devices: none -> 69.2 us  [per_device(): total = jnp.sum(lax.all_gather(projected, 'head'), axis=0)]
    psum x1 -> x0, waiting for transfers between devices: 46.8 us -> none  [per_device(): total = lax.psum(projected, 'head')]
    reduce_sum x0 -> x1, other arithmetic: none -> 5.79 us  [per_device(): total = jnp.sum(lax.all_gather(projected, 'head'), axis=0)]
  transfers between devices with their start and end apart: 13 -> 13, of which waited for: 3 -> 3; matrix products, arithmetic and copies ran while one was open for 16% -> 15% of each run, Pallas kernels for 0% -> 0%
where the time goes in v1:
time: 471 us; the launch traced here: 464 us
  waiting for transfers between devices  181 us (38%)
  blocking collectives  85.6 us (18%)
  local copies, waits for them, and re-layouts  62.8 us (13%)
  starting transfers between devices  54.1 us (11%)
  other arithmetic  34.6 us (7%)
  matrix products  30.6 us (6%)
  between operations  14.5 us (3%)
    reduce_scatter x1, waiting for transfers between devices, per_device(): lax.psum_scatter(partial_value.reshape(EXPERTS * CAP, model_width), 'head...  92 us
    all_to_all x1, blocking collectives, per_device(): lax.all_to_all(outgoing, 'tok', split_axis=0, concat_axis=0, tiled=True)  85.6 us
    all_gather x1, waiting for transfers between devices, per_device(): total = jnp.sum(lax.all_gather(projected, 'head'), axis=0)  69.2 us
    ppermute x8, starting transfers between devices, from_behind(): lax.ppermute(value, axis, [(source, source + steps) for source in range(l...  37.9 us
    all_to_all x1, waiting for transfers between devices, per_device(): lax.all_to_all(slot_cols.reshape(tok_count, local_experts * CAP, column_w...  20 us
    gather x1, local copies, waits for them, and re-layouts, per_device(): normed[source_row]  14.1 us
    unnamed x42, local copies, waits for them, and re-layouts  11.6 us
    all_to_all x1, starting transfers between devices, per_device(): lax.all_to_all(slot_cols.reshape(tok_count, local_experts * CAP, column_w...  9.83 us
  transfers between devices with their start and end apart: 13, of which 3 were waited for; matrix products, arithmetic and copies ran while one was open for 15% of the time, Pallas kernels for 0%

profile of v1, /device:TPU:8, one launch (start us, length us, event | category | flops | bytes accessed | tf_op | source)
XLA Modules:
  0.0 463.5 jit_solution(4671012141818722594)
XLA Ops:
  8.5 5.8 %collective-permute-start.4 = (bf16[256,512]{0,1:T(8,128)(2,1)S(1)}, bf16[256,512]{0,1:T(8,128)(2,1)S(1)}, u32[]{:S(2)}, u32[]{:S(2)}) collective-permute-start(bf16[256,512]{0,1:T(8,128)(2,1)S(1)} %copy.77), channel_id=1, source_target_pairs={{0,4},{1,5},{2,6},{3,7},{4,8},{5,9},{6,10},{7,11},{8,12},{9,13},{1... | collective-permute-start | bytes 786440 | tf_op jit(solution)/shard_map/ppermute | solution.py:18
  14.3 3.1 collective-permute-start.5
  17.3 4.5 collective-permute-start.6
  21.8 3.1 collective-permute-start.7
  25.0 6.5 %collective-permute-start = (bf16[256,512]{1,0:T(8,128)(2,1)}, bf16[256,512]{1,0:T(8,128)(2,1)}, u32[]{:S(2)}, u32[]{:S(2)}) collective-permute-start(bf16[256,512]{1,0:T(8,128)(2,1)} %param.18), channel_id=1, source_target_pairs={{0,4},{1,5},{2,6},{3,7},{4,8},{5,9},{6,10},{7,11},{8,12},{9,13},{1... | collective-permute-start | bytes 786440 | tf_op jit(solution)/shard_map/ppermute | solution.py:18
  34.0 9.6 %collective-permute-start.1 = (bf16[256,512]{1,0:T(8,128)(2,1)}, bf16[256,512]{1,0:T(8,128)(2,1)S(1)}, u32[]{:S(2)}, u32[]{:S(2)}) collective-permute-start(bf16[256,512]{1,0:T(8,128)(2,1)} %param.18), channel_id=1, source_target_pairs={{0,3},{1,4},{2,5},{3,6},{4,7},{5,8},{6,9},{7,10},{8,11},{9,12},{10... | collective-permute-start | bytes 786440 | tf_op jit(solution)/shard_map/ppermute | solution.py:18
  46.1 4.0 collective-permute-start.3
  56.9 2.4 copy.76
  59.3 3.5 exponential_reduce_fusion
  62.8 4.5 fusion.15
  67.3 3.7 fusion.75
  72.1 9.0 %reduce-window.6 = s32[32,8,128]{2,1,0:T(8,128)S(1)} reduce-window(s32[32,8,128]{2,1,0:T(8,128)S(1)} %fusion.42, s32[]{:T(128)} %constant.46.clone.1), window={size=1x1x128 pad=0_0x0_0x127_0}, to_apply=%region_5.6 | reduce-window | flops 4161536 | bytes 262148 | tf_op jit(solution)/shard_map/reduce-window
  81.9 4.8 %scatter_custom_fusion.1 = s32[1536]{0:T(1024)S(1)} fusion(s32[1024]{0:T(1024)S(1)} %bitcast.160, s32[1024]{0:T(1024)S(1)} %add_select_fusion.3, s32[]{:T(128)} %constant.46.clone.1), kind=kCustom, calls=%fused_computation.98 | custom fusion | bytes 6148 | tf_op jit(solution)/shard_map/scatter | solution.py:108
  86.7 4.3 scatter_custom_fusion
  91.1 69.2 %all-gather.3.cloned.1.call-done = f32[1024,2048]{1,0:T(8,128)} async-done(((f32[256,2048]{1,0:T(8,128)}), f32[1024,2048]{1,0:T(8,128)}) %all-gather.3.cloned.1.call-update) | async-done | bytes 8388624 | tf_op jit(solution)/shard_map/all_gather | solution.py:85
  160.4 5.8 %reduce_sum.57 = f32[256,2048]{1,0:T(8,128)} reduce(f32[4,256,2048]{2,1,0:T(8,128)} %bitcast.148, f32[]{:T(128)} %constant.91.clone.1), dimensions={0}, to_apply=%region_2.3 | reduce | flops 1572864 | bytes 10485764 | tf_op jit(solution)/shard_map/reduce_sum | solution.py:85
  171.0 14.1 %gather_fusion = bf16[1536,2048]{1,0:T(8,128)(2,1)} fusion(bf16[256,2048]{1,0:T(8,128)(2,1)} %multiply_convert_fusion, s32[2048]{0:T(1024)S(1)} %pad_clamp_fusion), kind=kCustom, calls=%fused_computation | custom fusion | bytes 12589056 | tf_op jit(solution)/shard_map/gather | solution.py:111
  185.1 3.3 broadcast_select_fusion
  188.3 85.6 %all_to_all.15 = bf16[32,1,48,2048]{3,2,1,0:T(8,128)(2,1)S(1)} all-to-all(bf16[32,1,48,2048]{3,2,1,0:T(8,128)(2,1)S(1)} %broadcast_select_fusion), channel_id=1, replica_groups=mesh['head'=4,'tok'=32] {'tok'}, dimensions={0} | all-to-all | bytes 12582912 | tf_op jit(solution)/shard_map/all_to_all | solution.py:115
  273.9 5.2 %fusion.7 = f32[32,1,48,2,352]{4,2,3,0,1:T(8,128)S(1)} fusion(bf16[1,2048,2,352]{1,3,2,0:T(8,128)(2,1)S(1)} %copy-done, bf16[32,1,48,2048]{3,2,1,0:T(8,128)(2,1)S(1)} %all_to_all.15), kind=kOutput, calls=%fused_computation.22 | convolution fusion | flops 4429185024 | bytes 13500416 | tf_op jit(solution)/shard_map/secd,edgf->secgf/dot_general | solution.py:22
  279.1 6.4 %fusion.12 = f32[32,48,2048]{2,1,0:T(8,128)} fusion(bf16[1,352,2048]{2,1,0:T(8,128)(2,1)S(1)} %copy-done.13, f32[32,1,48,2,352]{4,2,3,0,1:T(8,128)S(1)} %fusion.7), kind=kOutput, calls=%fused_computation.28 | convolution fusion | flops 2217836544 | bytes 18350080 | tf_op jit(solution)/shard_map/secf,efd->secd/dot_general | solution.py:24
  287.2 4.5 fusion.18
  291.7 2.4 convolution_multiply_fusion
  296.0 4.3 scatter_custom_fusion.3
  304.2 6.2 %all-to-all-start.2 = ((bf16[128,1,2,2,4,128]{5,4,3,2,1,0:T(4,128)(2,1)}), bf16[128,1,2,2,4,128]{5,4,3,2,1,0:T(4,128)(2,1)S(1)}, u32[]{:S(2)}, u32[]{:S(2)}) async-start(bf16[128,1,2,2,4,128]{5,4,3,2,1,0:T(4,128)(2,1)} %copy.93), calls=%async_computation.4 | async-start | bytes 1048576 | tf_op jit(solution)/shard_map/all_to_all | solution.py:170
  310.4 92.0 %reduce-scatter.5.cloned.1.call-done = f32[1536,512]{1,0:T(8,128)} async-done(((f32[1536,2048]{1,0:T(8,128)}), f32[1536,512]{1,0:T(8,128)}) %reduce-scatter.5.cloned.1.call-update) | async-done | bytes 3145744 | tf_op jit(solution)/shard_map/reduce_scatter | solution.py:121
  402.5 3.2 convert_element_type.57
  405.7 9.8 %all-to-all-start.1 = ((bf16[32,48,512]{2,1,0:T(8,128)(2,1)}), bf16[32,48,512]{2,1,0:T(8,128)(2,1)S(1)}, u32[]{:S(2)}, u32[]{:S(2)}) async-start(bf16[32,48,512]{2,1,0:T(8,128)(2,1)} %bitcast.33), calls=%async_computation.3 | async-start | bytes 3145728 | tf_op jit(solution)/shard_map/all_to_all | solution.py:129
  419.2 20.0 %all-to-all-done.1 = bf16[32,48,512]{2,1,0:T(8,128)(2,1)S(1)} async-done(((bf16[32,48,512]{2,1,0:T(8,128)(2,1)}), bf16[32,48,512]{2,1,0:T(8,128)(2,1)S(1)}, u32[]{:S(2)}, u32[]{:S(2)}) %all-to-all-start.1) | async-done | bytes 1572896 | tf_op jit(solution)/shard_map/all_to_all | solution.py:129
  441.4 7.2 %gather_fusion.1 = f32[1024,512]{1,0:T(8,128)} fusion(f32[1536,512]{1,0:T(8,128)} %bitcast_convert_fusion, s32[1024]{0:T(1024)S(1)} %broadcast_clamp_fusion), kind=kCustom, calls=%fused_computation.1 | custom fusion | bytes 4198400 | tf_op jit(solution)/shard_map/gather | solution.py:136
  448.7 3.1 reshape.311
  451.8 2.9 multiply_reduce_fusion
  (117 shorter events, 34.9 us)
Async XLA Ops:
  7.2 266.7 %copy-start = (bf16[1,2048,2,352]{1,3,2,0:T(8,128)(2,1)S(1)}, bf16[1,2048,2,352]{1,3,2,0:T(8,128)(2,1)}, u32[]{:S(2)}) copy-start(bf16[1,2048,2,352]{1,3,2,0:T(8,128)(2,1)} %param.22) | copy-start | bytes 8650756
  7.2 153.2 %all-gather.3.cloned.1.call-start = ((), (), s32[]{:S(2)}) async-start(), calls=%async_computation.7 | async-start | bytes 10485760 | tf_op jit(solution)/shard_map/all_gather | solution.py:85
  8.5 25.6 %collective-permute-start.4 = (bf16[256,512]{0,1:T(8,128)(2,1)S(1)}, bf16[256,512]{0,1:T(8,128)(2,1)S(1)}, u32[]{:S(2)}, u32[]{:S(2)}) collective-permute-start(bf16[256,512]{0,1:T(8,128)(2,1)S(1)} %copy.77), channel_id=1, source_target_pairs={{0,4},{1,5},{2,6},{3,7},{4,8},{5,9},{6,10},{7,11},{8,12},{9,13},{1... | collective-permute-start | bytes 786440 | tf_op jit(solution)/shard_map/ppermute | solution.py:18
  14.3 29.4 %collective-permute-start.5 = (bf16[256,512]{0,1:T(8,128)(2,1)S(1)}, bf16[256,512]{0,1:T(8,128)(2,1)}, u32[]{:S(2)}, u32[]{:S(2)}) collective-permute-start(bf16[256,512]{0,1:T(8,128)(2,1)S(1)} %copy.77), channel_id=1, source_target_pairs={{0,3},{1,4},{2,5},{3,6},{4,7},{5,8},{6,9},{7,10},{8,11},{9,12},{10... | collective-permute-start | bytes 786440 | tf_op jit(solution)/shard_map/ppermute | solution.py:18
  17.3 28.7 %collective-permute-start.6 = (bf16[256,512]{0,1:T(8,128)(2,1)S(1)}, bf16[256,512]{0,1:T(8,128)(2,1)}, u32[]{:S(2)}, u32[]{:S(2)}) collective-permute-start(bf16[256,512]{0,1:T(8,128)(2,1)S(1)} %copy.77), channel_id=1, source_target_pairs={{0,2},{1,3},{2,4},{3,5},{4,6},{5,7},{6,8},{7,9},{8,10},{9,11},{10,... | collective-permute-start | bytes 786440 | tf_op jit(solution)/shard_map/ppermute | solution.py:18
  21.8 29.2 %collective-permute-start.7 = (bf16[256,512]{0,1:T(8,128)(2,1)S(1)}, bf16[256,512]{0,1:T(8,128)(2,1)}, u32[]{:S(2)}, u32[]{:S(2)}) collective-permute-start(bf16[256,512]{0,1:T(8,128)(2,1)S(1)} %copy.77), channel_id=1, source_target_pairs={{0,1},{1,2},{2,3},{3,4},{4,5},{5,6},{6,7},{7,8},{8,9},{9,10},{10,1... | collective-permute-start | bytes 786440 | tf_op jit(solution)/shard_map/ppermute | solution.py:18
  25.0 27.1 %collective-permute-start = (bf16[256,512]{1,0:T(8,128)(2,1)}, bf16[256,512]{1,0:T(8,128)(2,1)}, u32[]{:S(2)}, u32[]{:S(2)}) collective-permute-start(bf16[256,512]{1,0:T(8,128)(2,1)} %param.18), channel_id=1, source_target_pairs={{0,4},{1,5},{2,6},{3,7},{4,8},{5,9},{6,10},{7,11},{8,12},{9,13},{1... | collective-permute-start | bytes 786440 | tf_op jit(solution)/shard_map/ppermute | solution.py:18
  34.0 19.9 %collective-permute-start.1 = (bf16[256,512]{1,0:T(8,128)(2,1)}, bf16[256,512]{1,0:T(8,128)(2,1)S(1)}, u32[]{:S(2)}, u32[]{:S(2)}) collective-permute-start(bf16[256,512]{1,0:T(8,128)(2,1)} %param.18), channel_id=1, source_target_pairs={{0,3},{1,4},{2,5},{3,6},{4,7},{5,8},{6,9},{7,10},{8,11},{9,12},{10... | collective-permute-start | bytes 786440 | tf_op jit(solution)/shard_map/ppermute | solution.py:18
  43.6 12.5 %copy-start.4 = (bf16[256,512]{1,0:T(8,128)(2,1)S(1)}, bf16[256,512]{1,0:T(8,128)(2,1)}, u32[]{:S(2)}) copy-start(bf16[256,512]{1,0:T(8,128)(2,1)} %param.18) | copy-start | bytes 786436
  43.6 11.0 %collective-permute-start.2 = (bf16[256,512]{1,0:T(8,128)(2,1)}, bf16[256,512]{1,0:T(8,128)(2,1)S(1)}, u32[]{:S(2)}, u32[]{:S(2)}) collective-permute-start(bf16[256,512]{1,0:T(8,128)(2,1)} %param.18), channel_id=1, source_target_pairs={{0,2},{1,3},{2,4},{3,5},{4,6},{5,7},{6,8},{7,9},{8,10},{9,11},{10,... | collective-permute-start | bytes 786440 | tf_op jit(solution)/shard_map/ppermute | solution.py:18
  46.1 9.3 %collective-permute-start.3 = (bf16[256,512]{1,0:T(8,128)(2,1)}, bf16[256,512]{1,0:T(8,128)(2,1)S(1)}, u32[]{:S(2)}, u32[]{:S(2)}) collective-permute-start(bf16[256,512]{1,0:T(8,128)(2,1)} %param.18), channel_id=1, source_target_pairs={{0,1},{1,2},{2,3},{3,4},{4,5},{5,6},{6,7},{7,8},{8,9},{9,10},{10,1... | collective-permute-start | bytes 786440 | tf_op jit(solution)/shard_map/ppermute | solution.py:18
  52.0 4.1 copy-start.6
  54.7 4.6 copy-start.14
  71.0 0.7 copy-start.7
  71.0 331.5 %reduce-scatter.5.cloned.1.call-start = ((), (), s32[]{:S(2)}) async-start(), calls=%async_computation.6 | async-start | bytes 15728640 | tf_op jit(solution)/shard_map/reduce_scatter | solution.py:121
  166.1 3.5 copy-start.9
  168.4 1.3 copy-start.3
  273.9 5.2 %copy-start.13 = (bf16[1,352,2048]{2,1,0:T(8,128)(2,1)S(1)}, bf16[1,352,2048]{2,1,0:T(8,128)(2,1)}, u32[]{:S(2)}) copy-start(bf16[1,352,2048]{2,1,0:T(8,128)(2,1)} %param.23) | copy-start | bytes 4325380
  285.5 0.7 copy-start.10
  285.5 0.7 copy-start.8
  285.6 1.3 copy-start.2
  285.6 169.2 %reduce-scatter.3.cloned.1.call-start = ((), (), s32[]{:S(2)}) async-start(), calls=%async_computation.5 | async-start | bytes 2621440 | tf_op jit(solution)/shard_map/reduce_scatter | solution.py:127
  287.2 4.5 copy-start.12
  294.1 1.0 copy-start.5
  304.2 101.5 %all-to-all-start.2 = ((bf16[128,1,2,2,4,128]{5,4,3,2,1,0:T(4,128)(2,1)}), bf16[128,1,2,2,4,128]{5,4,3,2,1,0:T(4,128)(2,1)S(1)}, u32[]{:S(2)}, u32[]{:S(2)}) async-start(bf16[128,1,2,2,4,128]{5,4,3,2,1,0:T(4,128)(2,1)} %copy.93), calls=%async_computation.4 | async-start | bytes 1048576 | tf_op jit(solution)/shard_map/all_to_all | solution.py:170
  405.7 9.8 %copy-start.11 = (f32[256,4]{0,1:T(4,128)S(1)}, f32[256,4]{0,1:T(4,128)}, u32[]{:S(2)}) copy-start(f32[256,4]{0,1:T(4,128)} %param.28) | copy-start | bytes 12292
  405.7 33.5 %all-to-all-start.1 = ((bf16[32,48,512]{2,1,0:T(8,128)(2,1)}), bf16[32,48,512]{2,1,0:T(8,128)(2,1)S(1)}, u32[]{:S(2)}, u32[]{:S(2)}) async-start(bf16[32,48,512]{2,1,0:T(8,128)(2,1)} %bitcast.33), calls=%async_computation.3 | async-start | bytes 3145728 | tf_op jit(solution)/shard_map/all_to_all | solution.py:129
  448.7 8.1 %copy-start.1 = (bf16[1,2048,2,352]{1,3,2,0:T(8,128)(2,1)S(1)}, bf16[1,2048,2,352]{1,3,2,0:T(8,128)(2,1)}, u32[]{:S(2)}) copy-start(bf16[1,2048,2,352]{1,3,2,0:T(8,128)(2,1)} %param.22) | copy-start | bytes 8650756
Sparse Core Ops, SparseCore 0:
  71.1 89.1 all-gather.2
  285.7 116.7 reduce-scatter.4
  404.9 46.0 reduce-scatter.2
